TPU v7x, 256 devices: a whole 4x4x8 slice. The times are simulated.
256 devices in a mesh: wide: 16 (over y_lo, z), row: 16 (over y_hi, x, core).
Axes of the slice: x: 4, y: 4 (y_hi: 2, y_lo: 2; y = y_hi * 2 + y_lo), z: 8, core: 2. Of those that a mesh axis runs over, the one named last changes fastest.
Arguments:
- hessian: float32 [18432, 18432], P('row', 'wide'), as said below
- weight: bfloat16 [4608, 18432], P('row', 'wide'), may hold values from -6 to 6
- pairs: int32 [2], replicated, may hold values from 0 to 47, as said below
Outputs:
- pruned_hessian: float32 [18432, 18432], P('row', 'wide')
- pruned_weight: bfloat16 [4608, 18432], P('row', 'wide')
Inputs may be any that keep to these rules, and one draw needn't show every extreme that they name: Two different head pairs, one of which is the last pair, 47. `hessian`: symmetric positive definite.
All inputs are finite; a program needn't handle non-finite values.
Results may differ from a plain program's by a relative error of at most 0.001.
Values may be sent and summed in bfloat16 or wider, within the bound.
A program may use at most 128 MiB of HBM per device.

v0:
```python
import functools

import jax
import jax.numpy as jnp
from jax import lax
from jax.experimental import pallas as pl
from jax.experimental.pallas import tpu as pltpu
from jax.sharding import PartitionSpec as P

HEAD = 192
PAIR = 2 * HEAD
NPAIRS = 48
N = 16
LAST = N - 1
MESH = pl.DeviceIdType.MESH
F32 = jnp.float32
BF16 = jnp.bfloat16
ANY = pl.BlockSpec(memory_space=pl.ANY)
VM = pl.BlockSpec(memory_space=pltpu.VMEM)


def remote(src, dst, send, recv, where):
    return pltpu.make_async_remote_copy(
        src_ref=src, dst_ref=dst, send_sem=send, recv_sem=recv,
        device_id=where, device_id_type=MESH,
    )


def greet_groups():
    row, wide = lax.axis_index("row"), lax.axis_index("wide")
    barrier = pltpu.get_barrier_semaphore()

    def body(d, _):
        pl.semaphore_signal(
            barrier, inc=1, device_id={"row": lax.rem(row + d, N)}, device_id_type=MESH
        )
        pl.semaphore_signal(
            barrier, inc=1, device_id={"wide": lax.rem(wide + d, N)}, device_id_type=MESH
        )
        return 0

    lax.fori_loop(1, N, body, 0)
    pl.semaphore_wait(barrier, 2 * (N - 1))


def scatter_kernel(root, cq, wq, pq, rq, c7, w7, r7,
                   ocq, owq, orq, oc7, ow7, or7, opv, pst, ssem, rsem, lsem):
    row, wide = lax.axis_index("row"), lax.axis_index("wide")
    greet_groups()
    at_wide, at_row = wide == root, row == root
    last_wide, last_row = wide == LAST, row == LAST

    def strip(m, columns):
        return r7.at[pl.ds(pl.multiple_of(2 * PAIR + 24 * m, 8), 24), columns]

    jobs = [
        (0, jnp.logical_and(at_row, at_wide), at_row, "wide", wide, lambda m: pq.at[m], pst.at[0]),
        (1, jnp.logical_and(at_row, last_wide), at_row, "wide", wide, lambda m: rq.at[m, :, pl.ds(2 * PAIR, PAIR)], pst.at[1]),
        (2, jnp.logical_and(last_row, last_wide), last_row, "wide", wide, lambda m: strip(m, pl.ds(2 * PAIR, PAIR)), pst.at[2]),
        (3, at_row, None, "row", row, lambda m: rq.at[m], orq),
        (4, last_row, None, "row", row, lambda m: strip(m, slice(None)), or7),
        (5, at_wide, None, "wide", wide, lambda m: cq.at[m], ocq),
        (6, last_wide, None, "wide", wide, lambda m: c7.at[m], oc7),
        (7, at_wide, None, "wide", wide, lambda m: wq.at[m], owq),
        (8, last_wide, None, "wide", wide, lambda m: w7.at[m], ow7),
    ]

    def spread(job, act):
        k, mine, _, axis, me, src, dst = job

        @pl.when(mine)
        def _():
            def body(m, _):
                @pl.when(m != me)
                def _():
                    copy = remote(src(m), dst, ssem.at[k, m], rsem.at[k], {axis: m})
                    copy.start() if act == "start" else copy.wait_send()

                @pl.when(m == me)
                def _():
                    copy = pltpu.make_async_copy(src(m), dst, lsem.at[k])
                    copy.start() if act == "start" else copy.wait()
                return 0

            lax.fori_loop(0, N, body, 0)

    def arrive(job):
        k, mine, group, axis, me, src, dst = job
        away = jnp.logical_not(mine)
        if group is not None:
            away = jnp.logical_and(away, group)

        @pl.when(away)
        def _():
            remote(src(0), dst, ssem.at[k, 0], rsem.at[k], {axis: 0}).wait_recv()

    for job in jobs:
        spread(job, "start")
    for job in jobs[:3]:
        arrive(job)
        spread(job, "drain")
    second = [(9, at_row, 0, 0, root), (10, at_row, 1, 0, root), (11, last_row, 2, 1, LAST)]

    def forward(item, act):
        k, mine, part, core, origin = item

        @pl.when(mine)
        def _():
            def body(h, _):
                m = 2 * h + core

                @pl.when(m != origin)
                def _():
                    copy = remote(pst.at[part], opv.at[part], ssem.at[k, m], rsem.at[k], {"row": m})
                    copy.start() if act == "start" else copy.wait_send()

                @pl.when(m == origin)
                def _():
                    copy = pltpu.make_async_copy(pst.at[part], opv.at[part], lsem.at[k])
                    copy.start() if act == "start" else copy.wait()
                return 0

            lax.fori_loop(0, N // 2, body, 0)

    for item in second:
        forward(item, "start")
    for item in second:
        k, mine, part, core, origin = item
        away = jnp.logical_and(jnp.logical_not(mine), lax.rem(row, 2) == core)

        @pl.when(away)
        def _():
            remote(pst.at[part], opv.at[part], ssem.at[k, 0], rsem.at[k], {"row": 0}).wait_recv()

    for job in jobs[3:]:
        arrive(job)
    for item in second:
        forward(item, "drain")
    for job in jobs[3:]:
        spread(job, "drain")


def piece(dtype, *shape):
    return jax.ShapeDtypeStruct(shape, dtype)


PIECES = [
    piece(BF16, 72, PAIR), piece(BF16, 18, PAIR), piece(F32, 24, 1152),
    piece(BF16, 72, PAIR), piece(BF16, 18, PAIR), piece(F32, 24, 1152),
    piece(F32, 3, 24, PAIR),
]


def scatter(root, *operands):
    outs = PIECES + [piece(F32, 3, 24, PAIR)]
    return pl.pallas_call(
        functools.partial(scatter_kernel, root),
        name=f"scatter_{root}",
        out_shape=outs,
        in_specs=[ANY] * 7,
        out_specs=[ANY] * 8,
        scratch_shapes=[
            pltpu.SemaphoreType.DMA((12, N)),
            pltpu.SemaphoreType.DMA((12,)),
            pltpu.SemaphoreType.DMA((12,)),
        ],
        compiler_params=pltpu.CompilerParams(collective_id=1 + root, has_side_effects=True),
    )(*operands)[:7]


def gather_kernel(cq, wq, rq, c7, w7, r7, pv,
                  gcq, gwq, grq, gc7, gw7, gr7, gpv,
                  lsem, xs, xr, zs, zr, hs, hr, ps, pr, fs, fr, ys, yr):
    row, wide = lax.axis_index("row"), lax.axis_index("wide")
    core, x, upper = lax.rem(row, 2), lax.rem(row // 2, 4), row // 8
    y, z = wide // 8, lax.rem(wide, 8)

    def on_wide(t, dz):
        return lax.rem(y + t, 2) * 8 + lax.rem(z + dz + 8, 8)

    def on_row(t, dx, other=0):
        chip = lax.rem(upper + t, 2) * 4 + lax.rem(x + dx + 4, 4)
        return chip * 2 + (core if other == 0 else 1 - core)

    neighbours = [
        {"wide": on_wide(0, 1)}, {"wide": on_wide(0, -1)}, {"wide": on_wide(1, 0)},
        {"row": on_row(0, 1)}, {"row": on_row(0, -1)}, {"row": on_row(1, 0)}, {"row": on_row(0, 0, 1)},
    ]
    barrier = pltpu.get_barrier_semaphore()
    for where in neighbours:
        pl.semaphore_signal(barrier, inc=1, device_id=where, device_id_type=MESH)
    pl.semaphore_wait(barrier, len(neighbours))
    partner = {"row": on_row(0, 0, 1)}

    pivots = [(0, pv.at[0], gpv.at[0], 0, 0), (1, pv.at[1], gpv.at[1], 1, 0), (2, pv.at[2], gpv.at[2], 0, 1)]
    columns = [(3, cq, gcq, 0, None), (4, c7, gc7, 1, None), (5, wq, gwq, 0, None), (6, w7, gw7, 1, None)]
    rows = [(7, rq, grq, 0, None), (8, r7, gr7, 1, None)]
    sign = (1, -1)

    def only(job, f):
        if job[4] is None:
            f()
        else:
            pl.when(core == job[4])(f)

    def local(job):
        k, src, dst = job[:3]
        return pltpu.make_async_copy(src, dst.at[row if k >= 7 else wide], lsem.at[k])

    def across(job):
        k, src, dst = job[:3]
        if k >= 7:
            return remote(src, dst.at[row], xs.at[k], xr.at[k], {"row": on_row(1, 0)})
        return remote(src, dst.at[wide], xs.at[k], xr.at[k], {"wide": on_wide(1, 0)})

    def crossed(job):
        k, src, dst = job[:3]
        if k >= 7:
            return remote(src, dst.at[on_row(1, 0)], xs.at[k], xr.at[k], {"row": on_row(1, 0)})
        return remote(src, dst.at[on_wide(1, 0)], xs.at[k], xr.at[k], {"wide": on_wide(1, 0)})

    def hop(job, t, way, d, arriving=False):
        k, src, dst = job[:3]
        s = sign[way]
        back = d if arriving else d - 1
        if k >= 7:
            block = dst.at[on_row(t, -s * back)]
            start = src if isinstance(d, int) and d == 1 and t == 0 else block
            return remote(start, block, hs.at[k - 7, t, way, d], hr.at[k - 7, t, way, d], {"row": on_row(0, s)})
        block = dst.at[on_wide(t, -s * back)]
        start = src if isinstance(d, int) and d == 1 and t == 0 else block
        return remote(start, block, zs.at[k, t, way, d], zr.at[k, t, way, d], {"wide": on_wide(0, s)})

    def share(job, t, dx, arriving=False):
        k, src, dst = job[:3]
        block = dst.at[on_row(t, dx, 1 if arriving else 0)]
        rel = dx + 2
        return remote(block, block, fs.at[k - 7, t, rel], fr.at[k - 7, t, rel], partner)

    def sides(job):
        return (0,) if job[0] == 4 else (0, 1)

    def step_across(job, dz, arriving=False):
        block = job[2].at[on_wide(1 if arriving else 0, dz)]
        return remote(block, block, ys.at[dz + 3], yr.at[dz + 3], {"wide": on_wide(1, 0)})

    def begin(job):
        local(job).start()
        across(job).start()
        hop(job, 0, 0, 1).start()
        hop(job, 0, 1, 1).start()

    def second(job):
        if len(sides(job)) == 2:
            crossed(job).wait_recv()
            hop(job, 1, 0, 1).start()
            hop(job, 1, 1, 1).start()

    def pass_on(job, d, ways):
        for t in sides(job):
            for way in (0, 1):
                hop(job, t, way, d, True).wait_recv()
                if ways == 2 or (ways == 1 and way == job[3]):
                    hop(job, t, way, d + 1).start()
                if len(sides(job)) == 1:
                    step_across(job, -sign[way] * d).start()

    def last(job, d):
        for t in sides(job):
            hop(job, t, job[3], d, True).wait_recv()
        if len(sides(job)) == 1:
            step_across(job, -sign[job[3]] * d).start()

    for job in pivots + columns + rows:
        only(job, lambda: begin(job))
    for job in pivots + columns:
        only(job, lambda: second(job))
    for job in rows:
        local(job).wait()
        share(job, 0, 0).start()
    for job in pivots + columns:
        only(job, lambda: pass_on(job, 1, 2))
    for job in rows:
        second(job)
        share(job, 1, 0).start()
    for job in pivots + columns:
        only(job, lambda: pass_on(job, 2, 2))
    for job in rows:
        pass_on(job, 1, 1)
        for t in (0, 1):
            share(job, t, -1).start()
            share(job, t, 1).start()
    for job in pivots + columns:
        only(job, lambda: pass_on(job, 3, 1))
    for job in pivots:
        def done(job=job):
            local(job).wait()
            last(job, 4)
            remote(job[2], job[2], ps.at[job[0]], pr.at[job[0]], partner).start()
        only(job, done)
    for job in rows:
        last(job, 2)
        for t in (0, 1):
            share(job, t, -2).start()
    for job in columns:
        local(job).wait()
        last(job, 4)

    def sent(job):
        across(job).wait_send()
        full = 2 if job[0] >= 7 else 4
        if len(sides(job)) == 1:
            crossed(job).wait_recv()
            for dz in (-1, 1, -2, 2, -3, 3, 4):
                step_across(job, dz, True).wait_recv()
                step_across(job, dz).wait_send()
        for t in sides(job):
            for way in (0, 1):
                for d in range(1, full + 1 if way == job[3] else full):
                    hop(job, t, way, d).wait_send()

    for job in pivots:
        def carried(job=job):
            sent(job)
            remote(job[2], job[2], ps.at[job[0]], pr.at[job[0]], partner).wait_send()
        only(job, carried)

        @pl.when(core != job[4])
        def _():
            remote(job[2], job[2], ps.at[job[0]], pr.at[job[0]], partner).wait_recv()
    for job in columns:
        sent(job)
    for job in rows:
        sent(job)
        for t in (0, 1):
            for dx in (0, -1, 1, -2):
                share(job, t, dx, True).wait_recv()
                share(job, t, dx).wait_send()


def gather(pieces):
    outs = [piece(p.dtype, N, *p.shape) for p in PIECES[:6]] + [piece(F32, 3, N, 24, PAIR)]
    return pl.pallas_call(
        gather_kernel,
        name="gather_panels",
        out_shape=outs,
        in_specs=[ANY] * 7,
        out_specs=[VM] * 7,
        scratch_shapes=[
            pltpu.SemaphoreType.DMA((9,)),
            pltpu.SemaphoreType.DMA((9,)),
            pltpu.SemaphoreType.DMA((9,)),
            pltpu.SemaphoreType.DMA((7, 2, 2, 5)),
            pltpu.SemaphoreType.DMA((7, 2, 2, 5)),
            pltpu.SemaphoreType.DMA((2, 2, 2, 3)),
            pltpu.SemaphoreType.DMA((2, 2, 2, 3)),
            pltpu.SemaphoreType.DMA((3,)),
            pltpu.SemaphoreType.DMA((3,)),
            pltpu.SemaphoreType.DMA((2, 2, 4)),
            pltpu.SemaphoreType.DMA((2, 2, 4)),
            pltpu.SemaphoreType.DMA((8,)),
            pltpu.SemaphoreType.DMA((8,)),
        ],
        compiler_params=pltpu.CompilerParams(collective_id=0, has_side_effects=True),
    )(*pieces)


def dot(a, b):
    return jnp.dot(a, b, preferred_element_type=F32)


def split(a):
    high = a.astype(BF16)
    return high, (a - high.astype(F32)).astype(BF16)


def dot3(a, b):
    ah, al = split(a)
    bh, bl = split(b)
    return dot(ah, bh) + (dot(ah, bl) + dot(al, bh))


def invert(a_ref, out_ref, s_ref, x_ref, r_ref):
    n = PAIR
    eye = (
        lax.broadcasted_iota(jnp.int32, (n, n), 0) == lax.broadcasted_iota(jnp.int32, (n, n), 1)
    ).astype(F32)
    a = a_ref[...]
    across = lax.rsqrt(jnp.sum(a * eye, axis=0, keepdims=True))
    down = lax.rsqrt(jnp.sum(a * eye, axis=1, keepdims=True))
    s = a * across * down
    sh, sl = split(s)
    s_ref[...] = jnp.concatenate([sh, sh, sl], 1)
    bound = jnp.max(jnp.sum(jnp.abs(s), axis=1, keepdims=True), axis=0, keepdims=True)
    start = 1.9 / bound
    x_ref[...] = start * eye
    r_ref[...] = eye - start * s

    def quick(_, c):
        r = r_ref[...].astype(BF16)
        x = x_ref[...]
        both = dot(jnp.concatenate([x.astype(BF16), r], 0), r)
        x_ref[...] = x + both[:n]
        r_ref[...] = both[n:]
        return c

    lax.fori_loop(0, 5, quick, 0)

    def careful(state):
        step, _ = state
        xh, xl = split(x_ref[...])
        r = eye - dot(s_ref[...], jnp.concatenate([xh, xl, xh], 0))
        size = jnp.max(jnp.sum(jnp.abs(r), axis=1, keepdims=True))
        lost = jnp.logical_and(step == 0, jnp.logical_not(size < 0.9))
        near = size < 0.25
        r_ref[...] = r

        @pl.when(lost)
        def _():
            x_ref[...] = eye / bound

        @pl.when(jnp.logical_and(jnp.logical_not(lost), jnp.logical_not(near)))
        def _():
            x_ref[...] = x_ref[...] + dot3(x_ref[...], r_ref[...])

        @pl.when(near)
        def _():
            x = x_ref[...]
            x_ref[...] = x + dot(x.astype(BF16), r_ref[...].astype(BF16))

        return step + 1, jnp.where(lost, 1.0, size)

    lax.while_loop(lambda s: jnp.logical_and(s[0] < 64, s[1] > 1e-3), careful, (0, 1.0))
    out_ref[...] = x_ref[...] * across * down


def finish_kernel(other, pv, b0, b1, cq, c7, wq, w7, h, w, oh, ow,
                  s_ref, x_ref, r_ref, g_ref, c_ref, m_ref, b_ref, x2_ref, w_ref, h_ref, sem):
    step = pl.program_id(0)

    @pl.when(step == 0)
    def _():
        loads = [pltpu.make_async_copy(b, b_ref.at[i], sem.at[i]) for i, b in enumerate((b0, b1))]
        loads.append(pltpu.make_async_copy(h, h_ref, sem.at[2]))
        for load in loads:
            load.start()

        def keep(i, value):
            high, low = split(value)
            m_ref[i] = jnp.concatenate([high, high, low], 1)

        def times(i, value):
            high, low = split(value)
            return dot(m_ref[i], jnp.concatenate([high, low, high], 0))

        invert(pv.at[0], g_ref, s_ref, x_ref, r_ref)
        keep(0, g_ref[...])
        keep(1, pv[1].T)
        t = times(0, pv[1])
        keep(3, t)
        c_ref[...] = pv[2] - times(1, t)
        invert(c_ref, g_ref, s_ref, x_ref, r_ref)
        keep(2, g_ref[...])
        for i, panel in enumerate((wq, w7)):
            for m in range(N):
                w_ref[i, 18 * m : 18 * m + 18, :] = panel[m].astype(F32)
        for load in loads:
            load.wait()

        first = times(0, b_ref[0])
        xb = times(2, b_ref[1] - times(1, first))
        xa = first - times(3, xb)
        for i, part in enumerate((xa, xb)):
            high, low = split(part)
            x2_ref[i * PAIR : (i + 1) * PAIR, :] = high
            x2_ref[(i + 2) * PAIR : (i + 3) * PAIR, :] = low
        panels = [w_ref[i].astype(BF16) for i in (0, 1)]
        change = dot(jnp.concatenate(panels * 2, 1), x2_ref[...])
        ow[...] = (w[...].astype(F32) - change).astype(BF16)

    strip = oh.shape[0]

    def pruned(origin, shape, dim):
        place = lax.broadcasted_iota(jnp.int32, shape, dim) + origin
        begin = other[0] * PAIR
        return jnp.where(
            jnp.logical_or(
                jnp.logical_and(place >= begin, place < begin + PAIR), place >= (NPAIRS - 1) * PAIR
            ),
            1, 0,
        )

    lines = lax.axis_index("row") * 1152 + step * strip

    gone = pruned(lines, (strip, 1), 0) + pruned(lax.axis_index("wide") * 1152, (1, 1152), 1)
    change = dot(jnp.concatenate([cq[...], c7[...]], 1), x2_ref[0 : 2 * PAIR, :])
    held = h_ref[pl.ds(pl.multiple_of(step * strip, 8), strip), :]
    oh[...] = jnp.where(gone > 0, 0.0, held - change)


def finish(other, pv, b0, b1, cq, c7, wq, w7, hessian, weight):
    steps = 4
    strip = 1152 // steps

    def whole(*shape):
        return pl.BlockSpec(shape, lambda g, o: (0,) * len(shape))

    def strips(columns):
        return pl.BlockSpec((strip, columns), lambda g, o: (g, 0))

    return pl.pallas_call(
        finish_kernel,
        name="finish",
        out_shape=[piece(F32, 1152, 1152), piece(BF16, 288, 1152)],
        grid_spec=pltpu.PrefetchScalarGridSpec(
            num_scalar_prefetch=1,
            grid=(steps,),
            in_specs=[
                whole(3, PAIR, PAIR), ANY, ANY, strips(PAIR), strips(PAIR),
                whole(N, 18, PAIR), whole(N, 18, PAIR), ANY, whole(288, 1152),
            ],
            out_specs=[strips(1152), whole(288, 1152)],
            scratch_shapes=[
                pltpu.VMEM((PAIR, 3 * PAIR), BF16),
                pltpu.VMEM((PAIR, PAIR), F32),
                pltpu.VMEM((PAIR, PAIR), F32),
                pltpu.VMEM((PAIR, PAIR), F32),
                pltpu.VMEM((PAIR, PAIR), F32),
                pltpu.VMEM((4, PAIR, 3 * PAIR), BF16),
                pltpu.VMEM((2, PAIR, 1152), F32),
                pltpu.VMEM((4 * PAIR, 1152), BF16),
                pltpu.VMEM((2, 288, PAIR), F32),
                pltpu.VMEM((1152, 1152), F32),
                pltpu.SemaphoreType.DMA((3,)),
            ],
        ),
    )(other, pv, b0, b1, cq, c7, wq, w7, hessian, weight)


def cut_kernel(block, hc, hr, hp, h7, wc, w7, ocq, owq, opq, orq, oc7, ow7):
    for m in range(N // 2):
        ocq[m] = hc[72 * m : 72 * m + 72, :].astype(BF16)
        oc7[m] = h7[72 * m : 72 * m + 72, :].astype(BF16)
        orq[m] = hr[24 * m : 24 * m + 24, :]
        opq[m] = hp[24 * m : 24 * m + 24, :]
    for src, out in ((wc, owq), (w7, ow7)):
        full = src[...].astype(F32)
        for m in range(N // 2):
            out[m] = full[18 * m : 18 * m + 18, :].astype(BF16)


def cut(block, hessian, weight):
    half = N // 2

    def out(*shape):
        return pl.BlockSpec((half, *shape), lambda g, b: (g, 0, 0))

    return pl.pallas_call(
        cut_kernel,
        name="cut",
        out_shape=[
            piece(BF16, N, 72, PAIR), piece(BF16, N, 18, PAIR), piece(F32, N, 24, PAIR),
            piece(F32, N, 24, 1152), piece(BF16, N, 72, PAIR), piece(BF16, N, 18, PAIR),
        ],
        grid_spec=pltpu.PrefetchScalarGridSpec(
            num_scalar_prefetch=1,
            grid=(2,),
            in_specs=[
                pl.BlockSpec((576, PAIR), lambda g, b: (g, b[0])),
                pl.BlockSpec((192, 1152), lambda g, b: (2 * b[0] + g, 0)),
                pl.BlockSpec((192, PAIR), lambda g, b: (2 * b[0] + g, b[0])),
                pl.BlockSpec((576, PAIR), lambda g, b: (g, 2)),
                pl.BlockSpec((144, PAIR), lambda g, b: (g, b[0])),
                pl.BlockSpec((144, PAIR), lambda g, b: (g, 2)),
            ],
            out_specs=[out(72, PAIR), out(18, PAIR), out(24, PAIR), out(24, 1152), out(72, PAIR), out(18, PAIR)],
        ),
    )(block, hessian, hessian, hessian, hessian, weight, weight)


def per_device(hessian, weight, pairs):
    tile = hessian.shape[0]
    per_tile = tile // PAIR
    other = jnp.minimum(pairs[0], pairs[1])
    root = other // per_tile
    block = (other % per_tile).reshape(1)
    cq, wq, pq, rq, c7, w7 = cut(block, hessian, weight)
    operands = (cq, wq, pq, rq, c7, w7, hessian)
    pieces = lax.switch(root, [functools.partial(scatter, i) for i in range(N)], *operands)
    gcq, gwq, grq, gc7, gw7, gr7, gpv = gather(pieces)

    return finish(
        other.reshape(1), gpv.reshape(3, PAIR, PAIR), grq.reshape(PAIR, tile), gr7.reshape(PAIR, tile),
        gcq.reshape(tile, PAIR), gc7.reshape(tile, PAIR), gwq, gw7, hessian, weight,
    )


def solution(mesh):
    return jax.shard_map(
        per_device,
        mesh=mesh,
        in_specs=(P("row", "wide"), P("row", "wide"), P()),
        out_specs=(P("row", "wide"), P("row", "wide")),
        check_vma=False,
    )
```

profile of v0, /device:TPU:16, one launch (start us, length us, event | category | flops | bytes accessed | tf_op | source)
XLA Modules:
  0.0 102.5 jit_solution(14075326154974736057)
XLA Ops:
  0.6 1.3 %fusion = (s32[1]{0:T(128)}, s32[1]{0:T(128)}) fusion(s32[2]{0:T(128)} %param.21), kind=kLoop, calls=%fused_computation | loop fusion | bytes 16 | tf_op jit(solution)/shard_map/slice | solution.py:584
  3.3 3.9 %cut.1 = (bf16[16,72,384]{2,1,0:T(8,128)(2,1)S(1)}, bf16[16,18,384]{2,1,0:T(8,128)(2,1)}, f32[16,24,384]{2,1,0:T(8,128)}, f32[16,24,1152]{2,1,0:T(8,128)S(1)}, b...) custom-call(s32[1]{0:T(128)} %bitcast.3.block, f32[1152,1152]{1,0:T(8,128)} %h.1, f32[1152,1152]{1,0:T(8,128)} %h.1, ...), custom_call_target="tpu_custom_call" | custom-call | tf_op jit(solution)/shard_map/cut/pallas_call | solution.py:558
  7.1 25.7 %conditional.1 = (bf16[72,384]{1,0:T(8,128)(2,1)}, bf16[18,384]{1,0:T(8,128)(2,1)}, f32[24,1152]{1,0:T(8,128)}, bf16[72,384]{1,0:T(8,128)(2,1)}, bf16[18,384]{1,...) conditional(s32[]{:T(128)} %clamp.3, ...), branch_computations={%region_0.1_spmd, %region_1.2_spmd, %region_2.3_spmd, %region_3.4_... | conditional | bytes 56 | solution.py:589
  7.1 25.5 %scatter_2.1 = (bf16[72,384]{1,0:T(8,128)(2,1)}, bf16[18,384]{1,0:T(8,128)(2,1)}, f32[24,1152]{1,0:T(8,128)}, bf16[72,384]{1,0:T(8,128)(2,1)}, bf16[18,384]{1,0:...) custom-call(bf16[16,72,384]{2,1,0:T(8,128)(2,1)S(1)} %get-tuple-element.252.cq, ...), custom_call_target="tpu_custom_call" | custom-call | tf_op jit(solution)/shard_map/cond/branch_2_fun/scatter_2/pallas_call | solution.py:156
  32.9 44.0 %gather_panels.1 = (bf16[16,72,384]{2,1,0:T(8,128)(2,1)}, bf16[16,18,384]{2,1,0:T(8,128)(2,1)}, f32[16,24,1152]{2,1,0:T(8,128)}, bf16[16,72,384]{2,1,0:T(8,128)(...) custom-call(bf16[72,384]{1,0:T(8,128)(2,1)} %get-tuple-element.476.cq, ...), custom_call_target="tpu_custom_call" | custom-call | tf_op jit(solution)/shard_map/gather_panels/pallas_call | solution.py:343
  76.9 25.5 %finish.1 = (f32[1152,1152]{1,0:T(8,128)}, bf16[288,1152]{1,0:T(8,128)(2,1)}) custom-call(s32[1]{0:T(128)S(6)} %min.4.other, f32[3,384,384]{2,1,0:T(8,128)} %bitcast.11, f32[384,1152]{1,0:T(8,128)} %bitcast.9, f32[384,1152]{1,0:T(8,128)} %bitcast.10, bf16[1152,384]{1,0:T(8,128)(2,1)} %bitcast.12, bf16[1152,384]{1,0:T(8,128)(2,1)} %bitcast.13, ...), custom_call_target="tpu_custom_call" | custom-call | tf_op jit(solution)/shard_map/finish/pallas_call | solution.py:511
where the time goes:
time: 103 us
  Pallas kernels  98.9 us (96%)
  between operations  2.14 us (2%)
  local copies, waits for them, and re-layouts  1.31 us (1%)
    pallas_call x1, Pallas kernels, gather(): pl.pallas_call(gather_kernel, name='gather_panels', out_shape=outs, in_sp...  44 us
    pallas_call x1, Pallas kernels, scatter(): pl.pallas_call(functools.partial(scatter_kernel, root), name=f'scatter_{r...  25.5 us
    pallas_call x1, Pallas kernels, finish(): pl.pallas_call(finish_kernel, name='finish', out_shape=[piece(F32, 1152,...  25.5 us
    pallas_call x1, Pallas kernels, cut(): pl.pallas_call(cut_kernel, name='cut', out_shape=[piece(BF16, N, 72, PAIR...  3.87 us

commit v1 on v0

--- a/solution.py
+++ b/solution.py
@@ -26,27 +26,27 @@
     )
 
 
-def greet_groups():
+def greet_holders(root):
     row, wide = lax.axis_index("row"), lax.axis_index("wide")
     barrier = pltpu.get_barrier_semaphore()
-
-    def body(d, _):
-        pl.semaphore_signal(
-            barrier, inc=1, device_id={"row": lax.rem(row + d, N)}, device_id_type=MESH
-        )
-        pl.semaphore_signal(
-            barrier, inc=1, device_id={"wide": lax.rem(wide + d, N)}, device_id_type=MESH
-        )
-        return 0
-
-    lax.fori_loop(1, N, body, 0)
-    pl.semaphore_wait(barrier, 2 * (N - 1))
+    peers = 0
+    for axis, me in (("wide", wide), ("row", row)):
+        for holder in sorted({root, LAST}):
+            @pl.when(me != holder)
+            def _():
+                pl.semaphore_signal(barrier, inc=1, device_id={axis: holder}, device_id_type=MESH)
+
+            peers = peers + jnp.where(me == holder, N - 1, 0)
+
+    @pl.when(peers > 0)
+    def _():
+        pl.semaphore_wait(barrier, peers)
 
 
 def scatter_kernel(root, cq, wq, pq, rq, c7, w7, r7,
                    ocq, owq, orq, oc7, ow7, or7, opv, pst, ssem, rsem, lsem):
     row, wide = lax.axis_index("row"), lax.axis_index("wide")
-    greet_groups()
+    greet_holders(root)
     at_wide, at_row = wide == root, row == root
     last_wide, last_row = wide == LAST, row == LAST
 

time: 103 us -> 102 us (level)
  the two profiles are of different devices: /device:TPU:16 before, /device:TPU:4 now
where the time goes in v1:
time: 102 us; the launch traced here: 101 us
  Pallas kernels  97.1 us (95%)
  between operations  2.16 us (2%)
  local copies, waits for them, and re-layouts  1.31 us (1%)
    pallas_call x1, Pallas kernels, gather(): pl.pallas_call(gather_kernel, name='gather_panels', out_shape=outs, in_sp...  48.3 us
    pallas_call x1, Pallas kernels, finish(): pl.pallas_call(finish_kernel, name='finish', out_shape=[piece(F32, 1152,...  25.5 us
    pallas_call x1, Pallas kernels, scatter(): pl.pallas_call(functools.partial(scatter_kernel, root), name=f'scatter_{r...  19.5 us
    pallas_call x1, Pallas kernels, cut(): pl.pallas_call(cut_kernel, name='cut', out_shape=[piece(BF16, N, 72, PAIR...  3.78 us

profile of v1, /device:TPU:4, one launch (start us, length us, event | category | flops | bytes accessed | tf_op | source)
XLA Modules:
  0.0 100.8 jit_solution(9974422153977569204)
XLA Ops:
  0.6 1.3 %fusion = (s32[1]{0:T(128)}, s32[1]{0:T(128)}) fusion(s32[2]{0:T(128)} %param.21), kind=kLoop, calls=%fused_computation | loop fusion | bytes 16 | tf_op jit(solution)/shard_map/slice | solution.py:584
  3.3 3.8 %cut.1 = (bf16[16,72,384]{2,1,0:T(8,128)(2,1)S(1)}, bf16[16,18,384]{2,1,0:T(8,128)(2,1)}, f32[16,24,384]{2,1,0:T(8,128)}, f32[16,24,1152]{2,1,0:T(8,128)S(1)}, b...) custom-call(s32[1]{0:T(128)} %bitcast.3.block, f32[1152,1152]{1,0:T(8,128)} %h.1, f32[1152,1152]{1,0:T(8,128)} %h.1, ...), custom_call_target="tpu_custom_call" | custom-call | tf_op jit(solution)/shard_map/cut/pallas_call | solution.py:558
  7.1 19.8 %conditional.1 = (bf16[72,384]{1,0:T(8,128)(2,1)}, bf16[18,384]{1,0:T(8,128)(2,1)}, f32[24,1152]{1,0:T(8,128)}, bf16[72,384]{1,0:T(8,128)(2,1)}, bf16[18,384]{1,...) conditional(s32[]{:T(128)} %clamp.3, ...), branch_computations={%region_0.1_spmd, %region_1.2_spmd, %region_2.3_spmd, %region_3.4_... | conditional | bytes 56 | solution.py:589
  7.1 19.5 %scatter_5.1 = (bf16[72,384]{1,0:T(8,128)(2,1)}, bf16[18,384]{1,0:T(8,128)(2,1)}, f32[24,1152]{1,0:T(8,128)}, bf16[72,384]{1,0:T(8,128)(2,1)}, bf16[18,384]{1,0:...) custom-call(bf16[16,72,384]{2,1,0:T(8,128)(2,1)S(1)} %get-tuple-element.294.cq, ...), custom_call_target="tpu_custom_call" | custom-call | tf_op jit(solution)/shard_map/cond/branch_5_fun/scatter_5/pallas_call | solution.py:156
  26.8 48.3 %gather_panels.1 = (bf16[16,72,384]{2,1,0:T(8,128)(2,1)}, bf16[16,18,384]{2,1,0:T(8,128)(2,1)}, f32[16,24,1152]{2,1,0:T(8,128)}, bf16[16,72,384]{2,1,0:T(8,128)(...) custom-call(bf16[72,384]{1,0:T(8,128)(2,1)} %get-tuple-element.476.cq, ...), custom_call_target="tpu_custom_call" | custom-call | tf_op jit(solution)/shard_map/gather_panels/pallas_call | solution.py:343
  75.1 25.5 %finish.1 = (f32[1152,1152]{1,0:T(8,128)}, bf16[288,1152]{1,0:T(8,128)(2,1)}) custom-call(s32[1]{0:T(128)S(6)} %min.4.other, f32[3,384,384]{2,1,0:T(8,128)} %bitcast.11, f32[384,1152]{1,0:T(8,128)} %bitcast.9, f32[384,1152]{1,0:T(8,128)} %bitcast.10, bf16[1152,384]{1,0:T(8,128)(2,1)} %bitcast.12, bf16[1152,384]{1,0:T(8,128)(2,1)} %bitcast.13, ...), custom_call_target="tpu_custom_call" | custom-call | tf_op jit(solution)/shard_map/finish/pallas_call | solution.py:511
